TPU v7x, 512 devices: a whole 4x8x8 slice. The times are simulated.
512 devices in a mesh: dp: 16 (over z, core), expert: 32 (over x, y).
Axes of the slice: x: 4, y: 8, z: 8, core: 2. Of those that a mesh axis runs over, the one named last changes fastest.
Arguments:
- layer_input: bfloat16 [1280, 4096], P('expert', 'dp'), may hold values from -6 to 6
- output_grad: bfloat16 [1280, 4096], P('expert', 'dp'), may hold values from -3 to 3
- route_ids: int32 [1280, 8], P('expert'), may hold values from 0 to 31, all different within a row; in each aligned block of 40 rows (0 to 39, 40 to 79, ...) at most 15 rows name the same one
- route_probs: bfloat16 [1280, 8], P('expert'), may hold values from 0.049804688 to 0.3984375
- gate_weight: bfloat16 [32, 4096, 1024], P('expert', 'dp'), may hold values from -0.09375 to 0.09375
- up_weight: bfloat16 [32, 4096, 1024], P('expert', 'dp'), may hold values from -0.09375 to 0.09375
- down_weight: bfloat16 [32, 1024, 4096], P('expert', None, 'dp'), may hold values from -0.1875 to 0.1875
Outputs:
- input_grad: bfloat16 [1280, 4096], P('expert', 'dp')
- prob_grad: bfloat16 [1280, 8], P('expert')
- gate_grad: bfloat16 [32, 4096, 1024], P('expert', 'dp')
- up_grad: bfloat16 [32, 4096, 1024], P('expert', 'dp')
- down_grad: bfloat16 [32, 1024, 4096], P('expert', None, 'dp')
Inputs may be any that keep to these rules, and one draw needn't show every extreme that they name: `route_ids`: each token names 8 different experts. In each aligned block of 40 tokens (the tokens of one index of the expert axis) at most 15 tokens name the same expert, and in every draw some expert is named by exactly 15 tokens of some block.
All inputs are finite; a program needn't handle non-finite values.
Results may differ from a plain program's by a relative error of at most 0.035.
Values may be sent and summed in bfloat16 or wider, within the bound.
A program may use at most 64 MiB of HBM per device.

v0:
```python
import jax
import jax.numpy as jnp
from jax import lax
from jax.sharding import PartitionSpec as P


def swiglu_back(gate_pre, up_pre, hidden_grad):
    sig_gate = jax.nn.sigmoid(gate_pre)
    active = (gate_pre * sig_gate * up_pre).astype(jnp.bfloat16)
    gate_delta = (hidden_grad * up_pre * sig_gate * (1.0 + gate_pre * (1.0 - sig_gate))).astype(
        jnp.bfloat16
    )
    up_delta = (hidden_grad * gate_pre * sig_gate).astype(jnp.bfloat16)
    return (active, gate_delta, up_delta)


def contract_last(left, right):
    return lax.dot_general(
        left, right, (((1,), (1,)), ((), ())), preferred_element_type=jnp.float32
    )


def on_device(
    layer_input, output_grad, route_ids, route_probs, gate_weight, up_weight, down_weight
):
    tok_count = layer_input.shape[0]
    width_part = layer_input.shape[1]
    chosen = route_ids.shape[1]
    experts = lax.axis_size("expert")
    capacity = 3 * tok_count * chosen // (2 * experts)
    row_count = experts * capacity
    cslots = jnp.arange(capacity, dtype=jnp.int32)
    expert_ids = jnp.arange(experts, dtype=jnp.int32)
    onehot = (route_ids[:, :, None] == expert_ids).astype(jnp.int32)
    member = jnp.sum(onehot, axis=1)
    before = jnp.cumsum(member, axis=0) - member
    pweight = jnp.sum(
        onehot.astype(jnp.float32) * route_probs.astype(jnp.float32)[:, :, None], axis=1
    )
    select = ((before[:, :, None] == cslots) & (member[:, :, None] > 0)).astype(jnp.bfloat16)
    send_x = jnp.einsum(
        "tec,td->ecd", select, layer_input, preferred_element_type=jnp.float32
    ).astype(jnp.bfloat16)
    send_g = jnp.einsum(
        "tec,td->ecd", select, output_grad, preferred_element_type=jnp.float32
    ).astype(jnp.bfloat16)
    send_p = jnp.einsum("tec,te->ec", select.astype(jnp.float32), pweight).astype(jnp.bfloat16)
    recv_x, recv_g, recv_p = (
        lax.all_to_all(send_x, "expert", split_axis=0, concat_axis=0, tiled=True),
        lax.all_to_all(send_g, "expert", split_axis=0, concat_axis=0, tiled=True),
        lax.all_to_all(send_p, "expert", split_axis=0, concat_axis=0, tiled=True),
    )
    rows_x = recv_x.reshape(row_count, width_part)
    rows_g = recv_g.reshape(row_count, width_part)
    rows_p = recv_p.reshape(row_count)
    gate_w = gate_weight[0]
    up_w = up_weight[0]
    down_w = down_weight[0]
    scaled = (rows_p.astype(jnp.float32)[:, None] * rows_g.astype(jnp.float32)).astype(jnp.bfloat16)
    gate_part = jnp.dot(rows_x, gate_w, preferred_element_type=jnp.float32)
    up_part = jnp.dot(rows_x, up_w, preferred_element_type=jnp.float32)
    grad_part = contract_last(scaled, down_w)
    gate_pre, up_pre, hidden_grad = (
        lax.psum(gate_part.astype(jnp.bfloat16), "dp").astype(jnp.float32),
        lax.psum(up_part.astype(jnp.bfloat16), "dp").astype(jnp.float32),
        lax.psum(grad_part.astype(jnp.bfloat16), "dp").astype(jnp.float32),
    )
    active, gate_delta, up_delta = swiglu_back(gate_pre, up_pre, hidden_grad)
    out_rows = jnp.dot(active, down_w, preferred_element_type=jnp.float32)
    dot_part = jnp.sum(rows_g.astype(jnp.float32) * out_rows, axis=1)
    gate_dot = lax.psum(dot_part, "dp").astype(jnp.bfloat16)
    down_grad = jnp.einsum("rf,rd->fd", active, scaled, preferred_element_type=jnp.float32).astype(
        jnp.bfloat16
    )[None]
    gate_grad = jnp.einsum(
        "rd,rf->df", rows_x, gate_delta, preferred_element_type=jnp.float32
    ).astype(jnp.bfloat16)[None]
    up_grad = jnp.einsum("rd,rf->df", rows_x, up_delta, preferred_element_type=jnp.float32).astype(
        jnp.bfloat16
    )[None]
    row_grad = (contract_last(gate_delta, gate_w) + contract_last(up_delta, up_w)).astype(
        jnp.bfloat16
    )
    back_x, back_p = (
        lax.all_to_all(
            row_grad.reshape(experts, capacity, width_part),
            "expert",
            split_axis=0,
            concat_axis=0,
            tiled=True,
        ),
        lax.all_to_all(
            gate_dot.reshape(experts, capacity), "expert", split_axis=0, concat_axis=0, tiled=True
        ),
    )
    input_sum = jnp.einsum("tec,ecd->td", select, back_x, preferred_element_type=jnp.float32)
    gate_table = jnp.einsum("tec,ec->te", select.astype(jnp.float32), back_p.astype(jnp.float32))
    input_grad = input_sum.astype(jnp.bfloat16)
    prob_grad = jnp.sum(onehot.astype(jnp.float32) * gate_table[:, None, :], axis=2).astype(
        jnp.bfloat16
    )
    return (input_grad, prob_grad, gate_grad, up_grad, down_grad)


def solution(mesh):
    placed = (
        P("expert", "dp"),
        P("expert", "dp"),
        P("expert", None),
        P("expert", None),
        P("expert", "dp", None),
        P("expert", "dp", None),
        P("expert", None, "dp"),
    )
    return jax.shard_map(
        on_device,
        mesh=mesh,
        in_specs=placed,
        out_specs=(
            P("expert", "dp"),
            P("expert", None),
            P("expert", "dp", None),
            P("expert", "dp", None),
            P("expert", None, "dp"),
        ),
        check_vma=False,
    )
```

profile of v0, /device:TPU:1, one launch (start us, length us, event | category | flops | bytes accessed | tf_op | source)
XLA Modules:
  0.0 362.6 jit_solution(10696455717776967576)
XLA Ops:
  7.2 0.8 convert_reduce_fusion
  8.2 0.9 convolution_convert_fusion.6
  9.3 20.0 %all_to_all.37 = bf16[32,15,256]{2,1,0:T(8,128)(2,1)S(1)} all-to-all(bf16[32,15,256]{2,1,0:T(8,128)(2,1)S(1)} %copy.51), channel_id=1, replica_groups=mesh['dp'=16,'expert'=32] {'expert'}, dimensions={0} | all-to-all | bytes 491520 | tf_op jit(solution)/shard_map/all_to_all | solution.py:49
  29.4 1.4 convolution_convert_fusion
  30.8 1.4 convolution_convert_fusion.1
  32.2 0.7 copy-done.6
  32.9 0.2 convolution_convert_fusion.7
  33.2 15.8 %all_to_all.38 = bf16[32,15,256]{2,1,0:T(8,128)(2,1)S(1)} all-to-all(bf16[32,15,256]{2,1,0:T(8,128)(2,1)S(1)} %copy.50), channel_id=1, replica_groups=mesh['dp'=16,'expert'=32] {'expert'}, dimensions={0} | all-to-all | bytes 491520 | tf_op jit(solution)/shard_map/all_to_all | solution.py:50
  49.1 106.6 %all-reduce.6.cloned.1.call-done = (bf16[480,1024]{1,0:T(8,128)(2,1)}, bf16[480,1024]{1,0:T(8,128)(2,1)}) async-done(((bf16[480,1024]{1,0:T(8,128)(2,1)}, bf16[480,1024]{1,0:T(8,128)(2,1)}), (bf16[480,1024]{1,0:T(8,128)(2,1)}, bf16[480,1024]{1,0:T(8,128)(2,1)})) %all-reduce.6.cloned.1.call-update) | async-done | bytes 1966096 | tf_op jit(solution)/shard_map/psum | solution.py:65
  155.7 2.2 fusion.3
  158.0 0.9 copy-done.1
  158.9 0.5 fusion.14
  159.4 23.9 %psum.31 = bf16[480]{0:T(512)(128)(2,1)S(1)} all-reduce(f32[480]{0:T(512)S(1)} %fusion.14), channel_id=1, replica_groups=mesh['dp'=16,'expert'=32] {'dp'}, use_global_device_ids=true, to_apply=%region_7.8 | all-reduce | flops 480 | bytes 2880 | tf_op jit(solution)/shard_map/psum | solution.py:71
  183.3 0.7 all_to_all.31
  184.1 9.3 %all-to-all-start.4 = ((bf16[32,1,15]{2,1,0:T(2,128)(2,1)}), bf16[32,1,15]{2,1,0:T(2,128)(2,1)S(1)}, u32[]{:S(2)}, u32[]{:S(2)}) async-start(bf16[32,1,15]{2,1,0:T(2,128)(2,1)} %all_to_all.31), calls=%async_computation.4 | async-start | bytes 32768 | tf_op jit(solution)/shard_map/all_to_all | solution.py:92
  193.5 8.5 %all-to-all-done.4 = bf16[32,1,15]{2,1,0:T(2,128)(2,1)S(1)} async-done(((bf16[32,1,15]{2,1,0:T(2,128)(2,1)}), bf16[32,1,15]{2,1,0:T(2,128)(2,1)S(1)}, u32[]{:S(2)}, u32[]{:S(2)}) %all-to-all-start.4) | async-done | bytes 992 | tf_op jit(solution)/shard_map/all_to_all | solution.py:92
  202.1 0.2 fusion.26
  202.3 0.6 fusion.33
  203.0 0.2 fusion.28
  203.4 11.6 %all_to_all.39 = bf16[32,1,15]{2,1,0:T(2,128)(2,1)S(1)} all-to-all(bf16[32,1,15]{2,1,0:T(2,128)(2,1)S(1)} %copy.49), channel_id=1, replica_groups=mesh['dp'=16,'expert'=32] {'expert'}, dimensions={0} | all-to-all | bytes 1920 | tf_op jit(solution)/shard_map/all_to_all | solution.py:51
  215.3 1.4 convolution_convert_fusion.2
  216.9 113.5 %all-reduce.4.cloned.1.call-done = bf16[480,1024]{1,0:T(8,128)(2,1)} async-done(((bf16[480,1024]{1,0:T(8,128)(2,1)}), bf16[480,1024]{1,0:T(8,128)(2,1)}) %all-reduce.4.cloned.1.call-update) | async-done | bytes 983056 | tf_op jit(solution)/shard_map/psum | solution.py:66
  330.4 2.8 fusion.9
  333.2 0.5 fusion.16
  333.7 0.5 fusion.13
  334.2 0.8 reshape.60
  335.0 9.4 %all-to-all-start.3 = ((bf16[32,15,256]{2,1,0:T(8,128)(2,1)}), bf16[32,15,256]{2,1,0:T(8,128)(2,1)}, u32[]{:S(2)}, u32[]{:S(2)}) async-start(bf16[32,15,256]{2,1,0:T(8,128)(2,1)} %reshape.60), calls=%async_computation.3 | async-start | bytes 524288 | tf_op jit(solution)/shard_map/all_to_all | solution.py:85
  344.4 2.6 fusion.12
  346.9 1.3 fusion.10
  348.2 1.3 fusion.11
  349.4 4.5 %all-to-all-done.3 = bf16[32,15,256]{2,1,0:T(8,128)(2,1)} async-done(((bf16[32,15,256]{2,1,0:T(8,128)(2,1)}), bf16[32,15,256]{2,1,0:T(8,128)(2,1)}, u32[]{:S(2)}, u32[]{:S(2)}) %all-to-all-start.3) | async-done | bytes 245792 | tf_op jit(solution)/shard_map/all_to_all | solution.py:85
  354.0 1.8 fusion.15
  (41 shorter events, 1.7 us)
Async XLA Ops:
  7.2 22.2 %copy-start = (bf16[1,256,1024]{2,1,0:T(8,128)(2,1)S(1)}, bf16[1,256,1024]{2,1,0:T(8,128)(2,1)}, u32[]{:S(2)}) copy-start(bf16[1,256,1024]{2,1,0:T(8,128)(2,1)} %param.11) | copy-start | bytes 1572868
  7.2 148.6 %all-reduce.6.cloned.1.call-start = ((), (), s32[]{:S(2)}) async-start(), calls=%async_computation.6 | async-start | bytes 3932160 | tf_op jit(solution)/shard_map/psum | solution.py:65
  29.4 1.4 copy-start.3
  32.2 0.7 copy-start.6
  49.1 108.8 %copy-start.4 = (f32[480,256]{1,0:T(8,128)}, f32[480,256]{1,0:T(8,128)S(1)}, u32[]{:S(2)}) copy-start(f32[480,256]{1,0:T(8,128)S(1)} %reshape.62) | copy-start | bytes 1474564
  155.7 3.2 copy-start.2
  157.9 1.0 copy-start.1
  158.9 34.5 %copy-start.8 = (bf16[40,8]{0,1:T(8,128)(2,1)S(1)}, bf16[40,8]{0,1:T(8,128)(2,1)}, u32[]{:S(2)}) copy-start(bf16[40,8]{0,1:T(8,128)(2,1)} %param.10) | copy-start | bytes 1924
  158.9 43.4 %copy-start.7 = (s32[40,8]{0,1:T(8,128)S(1)}, s32[40,8]{0,1:T(8,128)}, u32[]{:S(2)}) copy-start(s32[40,8]{0,1:T(8,128)} %param.9) | copy-start | bytes 3844
  184.1 17.9 %all-to-all-start.4 = ((bf16[32,1,15]{2,1,0:T(2,128)(2,1)}), bf16[32,1,15]{2,1,0:T(2,128)(2,1)S(1)}, u32[]{:S(2)}, u32[]{:S(2)}) async-start(bf16[32,1,15]{2,1,0:T(2,128)(2,1)} %all_to_all.31), calls=%async_computation.4 | async-start | bytes 32768 | tf_op jit(solution)/shard_map/all_to_all | solution.py:92
  193.3 137.0 %all-reduce.4.cloned.1.call-start = ((), (), s32[]{:S(2)}) async-start(), calls=%async_computation.5 | async-start | bytes 1966080 | tf_op jit(solution)/shard_map/psum | solution.py:66
  334.1 10.2 %copy-start.5 = (f32[480,256]{1,0:T(8,128)S(1)}, f32[480,256]{1,0:T(8,128)}, u32[]{:S(2)}) copy-start(f32[480,256]{1,0:T(8,128)} %copy-done.4) | copy-start | bytes 1474564
  335.0 19.0 %all-to-all-start.3 = ((bf16[32,15,256]{2,1,0:T(8,128)(2,1)}), bf16[32,15,256]{2,1,0:T(8,128)(2,1)}, u32[]{:S(2)}, u32[]{:S(2)}) async-start(bf16[32,15,256]{2,1,0:T(8,128)(2,1)} %reshape.60), calls=%async_computation.3 | async-start | bytes 524288 | tf_op jit(solution)/shard_map/all_to_all | solution.py:85
Sparse Core Ops, SparseCore 0:
  32.3 123.3 all-reduce.5
  216.8 113.5 all-reduce.3
where the time goes:
time: 366 us; the launch traced here: 363 us
  waiting for transfers between devices  233 us (64%)
  blocking collectives  71.3 us (19%)
  starting transfers between devices  18.7 us (5%)
  between operations  14.3 us (4%)
  matrix products  14 us (4%)
  other arithmetic  6.74 us (2%)
  local copies, waits for them, and re-layouts  4.39 us (1%)
    psum x1, waiting for transfers between devices, on_device(): lax.psum(grad_part.astype(jnp.bfloat16), 'dp').astype(jnp.float32)  114 us
    psum x1, waiting for transfers between devices, on_device(): lax.psum(up_part.astype(jnp.bfloat16), 'dp').astype(jnp.float32)  107 us
    psum x1, blocking collectives, on_device(): gate_dot = lax.psum(dot_part, 'dp').astype(jnp.bfloat16)  23.9 us
    all_to_all x1, blocking collectives, on_device(): lax.all_to_all(send_x, 'expert', split_axis=0, concat_axis=0, tiled=True)  20 us
    all_to_all x1, blocking collectives, on_device(): lax.all_to_all(send_g, 'expert', split_axis=0, concat_axis=0, tiled=True)  15.8 us
    all_to_all x1, blocking collectives, on_device(): lax.all_to_all(send_p, 'expert', split_axis=0, concat_axis=0, tiled=True)  11.6 us
    all_to_all x1, starting transfers between devices, on_device(): lax.all_to_all(row_grad.reshape(experts, capacity, width_part), 'expert',...  9.4 us
    all_to_all x1, starting transfers between devices, on_device(): lax.all_to_all(gate_dot.reshape(experts, capacity), 'expert', split_axis=...  9.26 us
  transfers between devices with their start and end apart: 4, of which 4 were waited for; matrix products, arithmetic and copies ran while one was open for 2% of the time, Pallas kernels for 0%

commit v1 on v0

v1 whole, which is shorter than its diff:
```python
import functools

import jax
import jax.numpy as jnp
from jax import lax
from jax.experimental import pallas as pl
from jax.experimental.pallas import tpu as pltpu
from jax.sharding import PartitionSpec as P

MESH = pl.DeviceIdType.MESH
BF = jnp.bfloat16
F32 = jnp.float32
BLK = 16
LANE = 128


def log2(n):
    return n.bit_length() - 1


def dot(a, b, ca=1, cb=0):
    return lax.dot_general(a, b, (((ca,), (cb,)), ((), ())), preferred_element_type=F32)


def iota(shape, dim):
    return lax.broadcasted_iota(jnp.int32, shape, dim)


def split_rows(block, width):
    rows = block.shape[0]
    x = block[:, :width].astype(F32)
    g = block[:, width:]
    head = x[:, :LANE].reshape(rows // BLK, BLK, LANE)
    shape = head.shape
    diag = iota(shape, 1) == iota(shape, 2)
    spread = jnp.broadcast_to(head[:, BLK - 1 :, :], shape)
    col = jnp.sum(jnp.where(diag, spread, 0.0), axis=2, keepdims=True).reshape(rows, 1)
    keep = (iota(x.shape, 0) & (BLK - 1)) != BLK - 1
    return jnp.where(keep, x, 0.0).astype(BF), g, col


def kernel(
    nx, ny, nz,
    x_ref, g_ref, ids_ref, prob_ref, gw_ref, uw_ref, dw_ref,
    xgrad_ref, pgrad_ref, ggrad_ref, ugrad_ref, dgrad_ref,
    tok, sel, send, recv, peer, part, rs_in, rs_out, hid, rgrad, back, pgw, puw, pdw, pcol, member_s,
    disp_s, disp_r, ret_s, ret_r, w_s, w_r, fwd_s, fwd_r, rs_s, rs_r, ag_s, ag_r, pt_s, pt_r,
):
    toks, width = x_ref.shape
    topk = ids_ref.shape[1]
    slots = nx * ny
    rows = slots * BLK
    chunks = ny // 2
    half = nx * BLK
    crows = 2 * half
    per = 2 * nx
    ha, hb = nz // 2, nz // 2 - 1
    lx = log2(nx)

    dp = lax.axis_index("dp")
    ex = lax.axis_index("expert")
    z, core = dp // 2, dp % 2
    mx, my = ex // ny, ex % ny
    s = 1 - 2 * core

    def zdev(step):
        return {"dp": ((z + step * s + nz) % nz) * 2 + core}

    fore, aft = zdev(1), zdev(-1)
    other = {"dp": z * 2 + 1 - core}

    def offset(q):
        c, b, dx = q // per, (q // nx) % 2, q % nx
        dy = jnp.where(b == 0, -c, c + 1)
        return dx, dy

    def target(q):
        dx, dy = offset(q)
        return {"expert": ((mx + dx) % nx) * ny + (my + dy + ny) % ny}

    def origin(q):
        dx, dy = offset(q)
        return {"expert": ((mx - dx + nx) % nx) * ny + (my - dy + ny) % ny}

    def remote(src, dst, ssem, rsem, dev):
        return pltpu.make_async_remote_copy(
            src_ref=src, dst_ref=dst, send_sem=ssem, recv_sem=rsem, device_id=dev, device_id_type=MESH
        )

    barrier = pltpu.get_barrier_semaphore()

    @pl.loop(1, slots)
    def _(q):
        pl.semaphore_signal(barrier, inc=1, device_id=target(q), device_id_type=MESH)

    for dev in (fore, aft, other):
        pl.semaphore_signal(barrier, inc=1, device_id=dev, device_id_type=MESH)

    q_lane = iota((toks, slots), 1)
    c_l, b_l, dx_l = q_lane >> (lx + 1), (q_lane >> lx) & 1, q_lane & (nx - 1)
    dy_l = jnp.where(b_l == 0, -c_l, c_l + 1)
    named = ((mx + dx_l) & (nx - 1)) * ny + ((my + dy_l) & (ny - 1))
    ids = ids_ref[...]
    prob = prob_ref[...].astype(F32)
    member = jnp.zeros((toks, slots), F32)
    weight = jnp.zeros((toks, slots), F32)
    for k in range(topk):
        hit = ids[:, k : k + 1] == named
        member = member + jnp.where(hit, 1.0, 0.0)
        weight = weight + jnp.where(hit, prob[:, k : k + 1], 0.0)
    lower = jnp.where(iota((toks, toks), 1) < iota((toks, toks), 0), 1.0, 0.0).astype(BF)
    before = dot(lower, member.astype(BF))
    slot = jnp.where(member > 0.0, before, -1.0)
    own_lane = (iota((slots, rows), 1) >> 4) == iota((slots, rows), 0)
    expand = jnp.where(own_lane, 1.0, 0.0).astype(BF)
    slot_x = dot(slot.astype(BF), expand)
    lane16 = (iota((toks, rows), 1) & (BLK - 1)).astype(F32)
    chosen = slot_x == lane16
    weight_x = dot(weight.astype(BF), expand)
    prob_vec = jnp.sum(jnp.where(chosen, weight_x, 0.0), axis=0, keepdims=True)
    spread = jnp.where((iota((rows, LANE), 0) & (BLK - 1)) == iota((rows, LANE), 1), 1.0, 0.0).astype(BF)
    prob_rows = dot(jnp.where(own_lane, prob_vec, 0.0).astype(BF), spread)
    scalar_lane = iota((slots, rows), 1) == iota((slots, rows), 0) * BLK + (BLK - 1)
    sel[0:slots, :] = jnp.where(scalar_lane, 1.0, 0.0).astype(BF)
    sel[slots : slots + toks, :] = jnp.where(chosen, 1.0, 0.0).astype(BF)
    tok[0:slots, :] = jnp.zeros((slots, 2 * width), BF)
    tok[0:slots, 0:LANE] = prob_rows.astype(BF)
    tok[slots : slots + toks, 0:width] = x_ref[...]
    tok[slots : slots + toks, width : 2 * width] = g_ref[...]
    packed = dot(sel[...], tok[...], 0, 0).astype(BF)
    send[...] = packed
    recv[0:BLK, :] = packed[0:BLK]

    pl.semaphore_wait(barrier, slots - 1 + 3)

    def w_copy(i):
        src, dst = ((gw_ref, pgw), (uw_ref, puw), (dw_ref, pdw))[i]
        return remote(src, dst, w_s.at[i], w_r.at[i], other)

    def block(q):
        return pl.ds(pl.multiple_of(q * BLK, BLK), BLK)

    def disp_copy(q):
        return remote(send.at[block(q)], recv.at[block(q)], disp_s.at[q], disp_r.at[q], target(q))

    def ret_copy(q):
        return remote(rgrad.at[block(q)], back.at[block(q)], ret_s.at[q], ret_r.at[q], origin(q))

    for i in range(3):
        w_copy(i).start()

    @pl.loop(1, slots)
    def _(q):
        disp_copy(q).start()

    def half_rows(k, h):
        return pl.ds(pl.multiple_of(k * crows + h * half, BLK), half)

    def fwd_copy(k):
        return remote(recv.at[half_rows(k, 1 - core)], peer.at[k], fwd_s.at[k], fwd_r.at[k], other)

    def zcol(step):
        j = (z + step * s + nz) % nz
        return j, pl.ds(pl.multiple_of(j * LANE, LANE), LANE)

    def rs_copy(k, i):
        return remote(rs_out.at[k, i], rs_in.at[k, i], rs_s.at[k, i], rs_r.at[k, i], fore if i < ha else aft)

    def rs_hop(k, h):
        for i, step, hops in ((h, ha - h, ha), (ha + h, h - hb, hb)):
            if h >= hops:
                continue
            v = part[k, :, :, zcol(step)[1]]
            if h > 0:
                rs_copy(k, i - 1).wait_recv()
                v = v + rs_in[k, i - 1].astype(F32)
            rs_out[k, i] = v.astype(BF)
            rs_copy(k, i).start()

    def hid_at(k, step):
        return hid.at[:, half_rows(k, core), zcol(step)[1]]

    def ag_copy(k, i):
        if i < ha:
            return remote(hid_at(k, -i), hid_at(k, -i), ag_s.at[k, i], ag_r.at[k, i], fore)
        return remote(hid_at(k, i - ha), hid_at(k, i - ha), ag_s.at[k, i], ag_r.at[k, i], aft)

    def pt_copy(k, step):
        j, _ = zcol(step)
        return remote(hid_at(k, step), hid_at(k, step), pt_s.at[k, j], pt_r.at[k, j], other)

    def arrive(k):
        @pl.loop(max(1, k * per), (k + 1) * per)
        def _(q):
            disp_copy(q).wait_recv()

        fwd_copy(k).start()

    def partials(k):
        fwd_copy(k).wait_recv()
        if k == 0:
            for i in range(3):
                w_copy(i).wait_recv()
        x0, g0, col = split_rows(recv[half_rows(k, core), :], width)
        x1, g1, _ = split_rows(peer[k], width)
        pcol[k] = jnp.broadcast_to(col, (half, LANE))
        part[k, 0] = dot(x0, gw_ref[...]) + dot(x1, pgw[...])
        part[k, 1] = dot(x0, uw_ref[...]) + dot(x1, puw[...])
        part[k, 2] = dot(g0, dw_ref[...], 1, 1) + dot(g1, pdw[...], 1, 1)
        rs_hop(k, 0)

    def swiglu(k):
        rs_copy(k, ha - 1).wait_recv()
        v = part[k, :, :, zcol(0)[1]] + rs_in[k, ha - 1].astype(F32)
        if hb > 0:
            rs_copy(k, ha + hb - 1).wait_recv()
            v = v + rs_in[k, ha + hb - 1].astype(F32)
        gate_pre, up_pre, raw = v[0], v[1], v[2]
        hidden_grad = raw * pcol[k]
        sig = 1.0 / (1.0 + jnp.exp(-gate_pre))
        active = gate_pre * sig * up_pre
        gate_delta = hidden_grad * up_pre * sig * (1.0 + gate_pre * (1.0 - sig))
        up_delta = hidden_grad * gate_pre * sig
        inner = jnp.sum(active * raw, axis=1, keepdims=True)
        shape = (half // BLK, BLK, LANE)
        diag = iota(shape, 1) == iota(shape, 2)
        spread = jnp.broadcast_to(inner, (half, LANE)).reshape(shape)
        line = jnp.sum(jnp.where(diag, spread, 0.0), axis=1, keepdims=True)
        high = line.astype(BF).astype(F32)
        last = iota(shape, 1) == BLK - 1

        def with_line(body, extra):
            return jnp.where(last, extra, body.reshape(shape)).reshape(half, LANE).astype(BF)

        at = (half_rows(k, core), zcol(0)[1])
        hid[(0, *at)] = with_line(active, high)
        hid[(1, *at)] = with_line(gate_delta, line - high)
        hid[(2, *at)] = up_delta.astype(BF)
        ag_copy(k, 0).start()
        if hb > 0:
            ag_copy(k, ha).start()
        pt_copy(k, 0).start()

    def ag_hop(k, h):
        for i, step, hops in ((h, -(h + 1), ha), (ha + h, h + 1, hb)):
            if h >= hops:
                continue
            ag_copy(k, i).wait_recv()
            if h + 1 < hops:
                ag_copy(k, i + 1).start()
            pt_copy(k, step).start()

    def give_back(k):
        for j in range(nz):
            at = hid.at[:, half_rows(k, 1 - core), pl.ds(j * LANE, LANE)]
            remote(at, at, pt_s.at[k, j], pt_r.at[k, j], other).wait_recv()
        mine = pl.ds(k * crows, crows)
        grad = dot(hid[1, mine, :], gw_ref[...], 1, 1) + dot(hid[2, mine, :], uw_ref[...], 1, 1)
        line = hid[0, mine, 0:LANE].astype(F32) + hid[1, mine, 0:LANE].astype(F32)
        for j in range(1, nz):
            at = slice(j * LANE, (j + 1) * LANE)
            line = line + hid[0, mine, at].astype(F32) + hid[1, mine, at].astype(F32)
        wide = jnp.concatenate([line] + [jnp.zeros_like(line)] * (width // LANE - 1), axis=1)
        last = (iota((crows, width), 0) & (BLK - 1)) == BLK - 1
        out = jnp.where(last, wide, grad).astype(BF)
        rgrad[mine, :] = out
        if k == 0:
            back[0:BLK, :] = out[0:BLK]

        @pl.loop(max(1, k * per), (k + 1) * per)
        def _(q):
            ret_copy(q).start()

    stages = [arrive, partials]
    stages += [functools.partial(lambda k, h: rs_hop(k, h), h=h) for h in range(1, ha)]
    stages += [swiglu]
    stages += [functools.partial(lambda k, h: ag_hop(k, h), h=h) for h in range(ha)]
    stages += [give_back]
    for tick in range(len(stages) + chunks - 1):
        for k in range(chunks):
            if 0 <= tick - k < len(stages):
                stages[tick - k](k)

    xs, gs, col = split_rows(recv[...], width)
    scaled = (gs.astype(F32) * col).astype(BF)
    ggrad_ref[...] = dot(xs, hid[1], 0, 0).astype(BF)
    ugrad_ref[...] = dot(xs, hid[2], 0, 0).astype(BF)
    dgrad_ref[...] = dot(hid[0], scaled, 0, 0).astype(BF)

    @pl.loop(1, slots)
    def _(q):
        ret_copy(q).wait_recv()

    picks = sel[slots : slots + toks, :]
    xgrad_ref[...] = dot(picks, back[...]).astype(BF)
    lines = back[...].astype(F32).reshape(slots, BLK, width)[:, BLK - 1, 0:LANE].astype(BF)
    line_x = jnp.where(own_lane, dot(lines, spread, 1, 1), 0.0)
    line_vec = jnp.sum(line_x, axis=0, keepdims=True)
    table = dot((picks.astype(F32) * line_vec).astype(BF), expand, 1, 1)
    result = jnp.zeros((toks, topk), F32)
    k_lane = iota((toks, topk), 1)
    for k in range(topk):
        hit = ids[:, k : k + 1] == named
        value = jnp.sum(jnp.where(hit, table, 0.0), axis=1, keepdims=True)
        result = jnp.where(k_lane == k, value, result)
    pgrad_ref[...] = result.astype(BF)

    for i in range(3):
        w_copy(i).wait_send()

    @pl.loop(1, slots)
    def _(q):
        disp_copy(q).wait_send()
        ret_copy(q).wait_send()

    for k in range(chunks):
        fwd_copy(k).wait_send()
        for i in range(ha + hb):
            rs_copy(k, i).wait_send()
            ag_copy(k, i).wait_send()
        for j in range(nz):
            at = hid.at[:, half_rows(k, core), pl.ds(j * LANE, LANE)]
            remote(at, at, pt_s.at[k, j], pt_r.at[k, j], other).wait_send()


def on_device(sizes, layer_input, output_grad, route_ids, route_probs, gate_weight, up_weight, down_weight):
    nx, ny, nz = sizes
    toks, width = layer_input.shape
    hidden = gate_weight.shape[2]
    topk = route_ids.shape[1]
    slots = nx * ny
    rows = slots * BLK
    chunks = ny // 2
    half = nx * BLK
    hops = nz - 1
    assert hidden == nz * LANE
    assert 3 * toks * topk // (2 * slots) < BLK
    vmem = pl.BlockSpec(memory_space=pltpu.VMEM)
    dma = pltpu.SemaphoreType.DMA
    outs = pl.pallas_call(
        functools.partial(kernel, nx, ny, nz),
        out_shape=(
            jax.ShapeDtypeStruct((toks, width), BF),
            jax.ShapeDtypeStruct((toks, topk), BF),
            jax.ShapeDtypeStruct((width, hidden), BF),
            jax.ShapeDtypeStruct((width, hidden), BF),
            jax.ShapeDtypeStruct((hidden, width), BF),
        ),
        in_specs=[vmem] * 7,
        out_specs=[vmem] * 5,
        scratch_shapes=[
            pltpu.VMEM((slots + toks, 2 * width), BF),
            pltpu.VMEM((slots + toks, rows), BF),
            pltpu.VMEM((rows, 2 * width), BF),
            pltpu.VMEM((rows, 2 * width), BF),
            pltpu.VMEM((chunks, half, 2 * width), BF),
            pltpu.VMEM((chunks, 3, half, hidden), F32),
            pltpu.VMEM((chunks, hops, 3, half, LANE), BF),
            pltpu.VMEM((chunks, hops, 3, half, LANE), BF),
            pltpu.VMEM((3, rows, hidden), BF),
            pltpu.VMEM((rows, width), BF),
            pltpu.VMEM((rows, width), BF),
            pltpu.VMEM((width, hidden), BF),
            pltpu.VMEM((width, hidden), BF),
            pltpu.VMEM((hidden, width), BF),
            pltpu.VMEM((chunks, half, LANE), F32),
            pltpu.VMEM((8, LANE), F32),
            dma((slots,)), dma((slots,)), dma((slots,)), dma((slots,)),
            dma((3,)), dma((3,)),
            dma((chunks,)), dma((chunks,)),
            dma((chunks, hops)), dma((chunks, hops)),
            dma((chunks, hops)), dma((chunks, hops)),
            dma((chunks, nz)), dma((chunks, nz)),
        ],
        compiler_params=pltpu.CompilerParams(
            collective_id=0, has_side_effects=True, vmem_limit_bytes=60 * 1024 * 1024
        ),
    )(
        layer_input, output_grad, route_ids, route_probs,
        gate_weight[0], up_weight[0], down_weight[0],
    )
    xgrad, pgrad, ggrad, ugrad, dgrad = outs
    return (xgrad, pgrad, ggrad[None], ugrad[None], dgrad[None])


def solution(mesh, sizes=(4, 8, 8)):
    placed = (
        P("expert", "dp"),
        P("expert", "dp"),
        P("expert", None),
        P("expert", None),
        P("expert", "dp", None),
        P("expert", "dp", None),
        P("expert", None, "dp"),
    )
    return jax.shard_map(
        functools.partial(on_device, sizes),
        mesh=mesh,
        in_specs=placed,
        out_specs=(
            P("expert", "dp"),
            P("expert", None),
            P("expert", "dp", None),
            P("expert", "dp", None),
            P("expert", None, "dp"),
        ),
        check_vma=False,
    )
```

time: 366 us -> 91.9 us (0.25)
  waiting for transfers between devices: 233 us -> 0 us
  Pallas kernels: 0 us -> 82.9 us
  blocking collectives: 71.3 us -> 0 us
  starting transfers between devices: 18.7 us -> 0 us
  matrix products: 14 us -> 0 us
  between operations: 14.3 us -> 0.66 us
  other arithmetic: 6.74 us -> 0 us
    psum x2 -> x0, waiting for transfers between devices: 220 us -> none  [the longest x1 114 us: on_device(): lax.psum(grad_part.astype(jnp.bfloat16), 'dp').astype(jnp.float32)]
    pallas_call x0 -> x1, Pallas kernels: none -> 82.9 us  [on_device(): pl.pallas_call(functools.partial(kernel, nx, ny, nz), out_shape=(jax.Shap...]
    all_to_all x3 -> x0, blocking collectives: 47.4 us -> none  [the longest x1 20 us: on_device(): lax.all_to_all(send_x, 'expert', split_axis=0, concat_axis=0, tiled=True)]
    psum x1 -> x0, blocking collectives: 23.9 us -> none  [on_device(): gate_dot = lax.psum(dot_part, 'dp').astype(jnp.bfloat16)]
    all_to_all x2 -> x0, starting transfers between devices: 18.7 us -> none  [the longest x1 9.4 us: on_device(): lax.all_to_all(row_grad.reshape(experts, capacity, width_part), 'expert',...]
    dot_general x14 -> x0, matrix products: 14 us -> none  [the longest x1 2.56 us: on_device(): jnp.einsum('rf,rd->fd', active, scaled, preferred_element_type=jnp.float32)]
    all_to_all x2 -> x0, waiting for transfers between devices: 13 us -> none  [the longest x1 8.47 us: on_device(): lax.all_to_all(gate_dot.reshape(experts, capacity), 'expert', split_axis=...]
    unnamed x18 -> x17, local copies, waits for them, and re-layouts: 1.69 us -> 7.96 us
  transfers between devices with their start and end apart: 4 -> 0, of which waited for: 4 -> 0; matrix products, arithmetic and copies ran while one was open for 2% -> 0% of each run, Pallas kernels for 0% -> 0%
where the time goes in v1:
time: 91.9 us; the launch traced here: 91.5 us
  Pallas kernels  82.9 us (90%)
  local copies, waits for them, and re-layouts  7.96 us (9%)
    pallas_call x1, Pallas kernels, on_device(): pl.pallas_call(functools.partial(kernel, nx, ny, nz), out_shape=(jax.Shap...  82.9 us
    unnamed x17, local copies, waits for them, and re-layouts  7.96 us

profile of v1, /device:TPU:1, one launch (start us, length us, event | category | flops | bytes accessed | tf_op | source)
XLA Modules:
  0.0 91.5 jit_solution(16734290781172738818)
XLA Ops:
  0.6 0.0 copy-start.4
  0.6 0.7 copy-done.4
  1.3 0.0 copy-start.3
  1.3 0.7 copy.13.prob_ref
  2.0 0.0 copy-done.3
  2.0 0.7 copy.12.ids_ref
  2.7 82.9 %shard_map.110 = (bf16[40,256]{1,0:T(8,128)(2,1)}, bf16[40,8]{1,0:T(8,128)(2,1)}, bf16[256,1024]{1,0:T(8,128)(2,1)}, bf16[256,1024]{1,0:T(8,128)(2,1)}, bf16[1024,256]{1,0:T(8,128)(2,1)}) custom-call(bf16[40,256]{1,0:T(8,128)(2,1)} %x_ref.1, bf16[40,256]{1,0:T(8,128)(2,1)} %g_ref.1, s32[40,8]{1,0:T(8,128)} %copy.12.ids_ref, bf16[40,8]{1,0:T(8,128)(2,1)} %copy.13.prob_ref, ...), custom_call_target="tpu_custom_call" | custom-call | tf_op jit(solution)/shard_map/pallas_call | solution.py:340
  85.6 0.0 copy-start.2
  85.6 1.4 %copy.14 = bf16[40,8]{0,1:T(8,128)(2,1)} copy(bf16[40,8]{1,0:T(8,128)(2,1)} %get-tuple-element.16) | data formatting | bytes 1280
  87.0 0.0 copy-done.2
  87.0 0.6 copy.19
  87.6 0.0 copy-start.1
  87.6 1.9 %copy.20 = bf16[1,256,1024]{2,1,0:T(8,128)(2,1)} copy(bf16[1,256,1024]{2,1,0:T(8,128)(2,1)} %bitcast.11) | data formatting | bytes 1048576
  89.5 0.0 copy-done.1
  89.5 0.0 copy-start
  89.5 0.8 copy.21
  90.3 0.4 copy-done
  90.7 0.8 copy.22
Async XLA Ops:
  0.6 0.7 copy-start.4
  1.3 0.7 copy-start.3
  85.6 1.4 %copy-start.2 = (bf16[40,256]{1,0:T(8,128)(2,1)S(1)}, bf16[40,256]{1,0:T(8,128)(2,1)}, u32[]{:S(2)}) copy-start(bf16[40,256]{1,0:T(8,128)(2,1)} %get-tuple-element.25) | copy-start | bytes 61444
  87.6 1.9 %copy-start.1 = (bf16[256,1024]{1,0:T(8,128)(2,1)S(1)}, bf16[256,1024]{1,0:T(8,128)(2,1)}, u32[]{:S(2)}) copy-start(bf16[256,1024]{1,0:T(8,128)(2,1)} %get-tuple-element.13) | copy-start | bytes 1572868
  89.5 1.2 %copy-start = (bf16[1024,256]{1,0:T(8,128)(2,1)S(1)}, bf16[1024,256]{1,0:T(8,128)(2,1)}, u32[]{:S(2)}) copy-start(bf16[1024,256]{1,0:T(8,128)(2,1)} %get-tuple-element.14) | copy-start | bytes 1572868

commit v2 on v1

--- a/solution.py
+++ b/solution.py
@@ -12,6 +12,12 @@
 F32 = jnp.float32
 BLK = 16
 LANE = 128
+PLAN = (
+    (0, 0), (1, 0), (0, 1), (2, 0), (1, 1), (3, 0), (0, 2), (4, 0), (2, 1), (1, 2), (5, 0), (3, 1), (2, 2), (0, 3),
+    (6, 0), (1, 3), (4, 1), (3, 2), (2, 3), (7, 0), (5, 1), (4, 2), (3, 3), (8, 0), (6, 1), (5, 2), (4, 3),
+    (9, 0), (7, 1), (6, 2), (5, 3), (8, 1), (7, 2), (6, 3), (10, 0), (9, 1), (8, 2), (7, 3), (10, 1), (9, 2), (8, 3),
+    (10, 2), (9, 3), (10, 3),
+)
 
 
 def log2(n):
@@ -41,13 +47,14 @@
 
 def kernel(
     nx, ny, nz,
-    x_ref, g_ref, ids_ref, prob_ref, gw_ref, uw_ref, dw_ref,
-    xgrad_ref, pgrad_ref, ggrad_ref, ugrad_ref, dgrad_ref,
-    tok, sel, send, recv, peer, part, rs_in, rs_out, hid, rgrad, back, pgw, puw, pdw, pcol, member_s,
+    x_ref, g_ref, ids_ref, prob_ref, gate_hbm, up_hbm, down_hbm,
+    xgrad_ref, pgrad_ref, ggrad_hbm, ugrad_hbm, dgrad_hbm,
+    tok, sel, send, recv, peer, part, rs_in, rs_out, hid, rgrad, back, pgw, puw, pdw, pcol,
+    gw_ref, uw_ref, dw_ref, ggrad_ref, ugrad_ref, dgrad_ref, in_s, out_s,
     disp_s, disp_r, ret_s, ret_r, w_s, w_r, fwd_s, fwd_r, rs_s, rs_r, ag_s, ag_r, pt_s, pt_r,
 ):
     toks, width = x_ref.shape
-    topk = ids_ref.shape[1]
+    topk = ids_ref.shape[0]
     slots = nx * ny
     rows = slots * BLK
     chunks = ny // 2
@@ -87,6 +94,15 @@
             src_ref=src, dst_ref=dst, send_sem=ssem, recv_sem=rsem, device_id=dev, device_id_type=MESH
         )
 
+    loads = ((gate_hbm, gw_ref), (up_hbm, uw_ref), (down_hbm, dw_ref))
+    stores = ((ggrad_ref, ggrad_hbm), (ugrad_ref, ugrad_hbm), (dgrad_ref, dgrad_hbm))
+
+    def load(i):
+        return pltpu.make_async_copy(*loads[i], in_s.at[i])
+
+    def store(i):
+        return pltpu.make_async_copy(*stores[i], out_s.at[i])
+
     barrier = pltpu.get_barrier_semaphore()
 
     @pl.loop(1, slots)
@@ -96,12 +112,16 @@
     for dev in (fore, aft, other):
         pl.semaphore_signal(barrier, inc=1, device_id=dev, device_id_type=MESH)
 
+    for i in range(3):
+        load(i).start()
+
     q_lane = iota((toks, slots), 1)
     c_l, b_l, dx_l = q_lane >> (lx + 1), (q_lane >> lx) & 1, q_lane & (nx - 1)
     dy_l = jnp.where(b_l == 0, -c_l, c_l + 1)
-    named = ((mx + dx_l) & (nx - 1)) * ny + ((my + dy_l) & (ny - 1))
-    ids = ids_ref[...]
-    prob = prob_ref[...].astype(F32)
+    named = (((mx + dx_l) & (nx - 1)) * ny + ((my + dy_l) & (ny - 1))).astype(F32)
+    eye = jnp.where(iota((toks, toks), 0) == iota((toks, toks), 1), 1.0, 0.0).astype(BF)
+    ids = dot(eye, ids_ref[...].astype(F32).astype(BF), 1, 1)
+    prob = dot(eye, prob_ref[...], 1, 1)
     member = jnp.zeros((toks, slots), F32)
     weight = jnp.zeros((toks, slots), F32)
     for k in range(topk):
@@ -134,7 +154,7 @@
     pl.semaphore_wait(barrier, slots - 1 + 3)
 
     def w_copy(i):
-        src, dst = ((gw_ref, pgw), (uw_ref, puw), (dw_ref, pdw))[i]
+        src, dst = ((gate_hbm, pgw), (up_hbm, puw), (down_hbm, pdw))[i]
         return remote(src, dst, w_s.at[i], w_r.at[i], other)
 
     def block(q):
@@ -200,6 +220,7 @@
         fwd_copy(k).wait_recv()
         if k == 0:
             for i in range(3):
+                load(i).wait()
                 w_copy(i).wait_recv()
         x0, g0, col = split_rows(recv[half_rows(k, core), :], width)
         x1, g1, _ = split_rows(peer[k], width)
@@ -276,16 +297,17 @@
     stages += [swiglu]
     stages += [functools.partial(lambda k, h: ag_hop(k, h), h=h) for h in range(ha)]
     stages += [give_back]
-    for tick in range(len(stages) + chunks - 1):
-        for k in range(chunks):
-            if 0 <= tick - k < len(stages):
-                stages[tick - k](k)
+    for stage, k in PLAN:
+        stages[stage](k)
 
     xs, gs, col = split_rows(recv[...], width)
     scaled = (gs.astype(F32) * col).astype(BF)
     ggrad_ref[...] = dot(xs, hid[1], 0, 0).astype(BF)
+    store(0).start()
     ugrad_ref[...] = dot(xs, hid[2], 0, 0).astype(BF)
+    store(1).start()
     dgrad_ref[...] = dot(hid[0], scaled, 0, 0).astype(BF)
+    store(2).start()
 
     @pl.loop(1, slots)
     def _(q):
@@ -303,9 +325,10 @@
         hit = ids[:, k : k + 1] == named
         value = jnp.sum(jnp.where(hit, table, 0.0), axis=1, keepdims=True)
         result = jnp.where(k_lane == k, value, result)
-    pgrad_ref[...] = result.astype(BF)
+    pgrad_ref[...] = dot(result.astype(BF), eye, 0, 0).astype(BF)
 
     for i in range(3):
+        store(i).wait()
         w_copy(i).wait_send()
 
     @pl.loop(1, slots)
@@ -321,6 +344,20 @@
         for j in range(nz):
             at = hid.at[:, half_rows(k, core), pl.ds(j * LANE, LANE)]
             remote(at, at, pt_s.at[k, j], pt_r.at[k, j], other).wait_send()
+
+
+def copy_out(*refs):
+    n = (len(refs) - 2) // 3
+    srcs, dsts, held = refs[:n], refs[n : 2 * n], refs[2 * n : 3 * n]
+    ins = [pltpu.make_async_copy(srcs[i], held[i], refs[3 * n].at[i]) for i in range(n)]
+    outs = [pltpu.make_async_copy(held[i], dsts[i], refs[3 * n + 1].at[i]) for i in range(n)]
+    for i in range(n):
+        ins[i].start()
+    for i in range(n):
+        ins[i].wait()
+        outs[i].start()
+    for i in range(n):
+        outs[i].wait()
 
 
 def on_device(sizes, layer_input, output_grad, route_ids, route_probs, gate_weight, up_weight, down_weight):
@@ -335,19 +372,22 @@
     hops = nz - 1
     assert hidden == nz * LANE
     assert 3 * toks * topk // (2 * slots) < BLK
+    assert (chunks, nz) == (4, 8)
     vmem = pl.BlockSpec(memory_space=pltpu.VMEM)
+    anyw = pl.BlockSpec(memory_space=pl.ANY)
     dma = pltpu.SemaphoreType.DMA
+    out_shape = (
+        jax.ShapeDtypeStruct((toks, width), BF),
+        jax.ShapeDtypeStruct((topk, toks), BF),
+        jax.ShapeDtypeStruct((width, hidden), BF),
+        jax.ShapeDtypeStruct((width, hidden), BF),
+        jax.ShapeDtypeStruct((hidden, width), BF),
+    )
     outs = pl.pallas_call(
         functools.partial(kernel, nx, ny, nz),
-        out_shape=(
-            jax.ShapeDtypeStruct((toks, width), BF),
-            jax.ShapeDtypeStruct((toks, topk), BF),
-            jax.ShapeDtypeStruct((width, hidden), BF),
-            jax.ShapeDtypeStruct((width, hidden), BF),
-            jax.ShapeDtypeStruct((hidden, width), BF),
-        ),
-        in_specs=[vmem] * 7,
-        out_specs=[vmem] * 5,
+        out_shape=out_shape,
+        in_specs=[vmem] * 4 + [anyw] * 3,
+        out_specs=[vmem] * 2 + [anyw] * 3,
         scratch_shapes=[
             pltpu.VMEM((slots + toks, 2 * width), BF),
             pltpu.VMEM((slots + toks, rows), BF),
@@ -364,7 +404,13 @@
             pltpu.VMEM((width, hidden), BF),
             pltpu.VMEM((hidden, width), BF),
             pltpu.VMEM((chunks, half, LANE), F32),
-            pltpu.VMEM((8, LANE), F32),
+            pltpu.VMEM((width, hidden), BF),
+            pltpu.VMEM((width, hidden), BF),
+            pltpu.VMEM((hidden, width), BF),
+            pltpu.VMEM((width, hidden), BF),
+            pltpu.VMEM((width, hidden), BF),
+            pltpu.VMEM((hidden, width), BF),
+            dma((3,)), dma((3,)),
             dma((slots,)), dma((slots,)), dma((slots,)), dma((slots,)),
             dma((3,)), dma((3,)),
             dma((chunks,)), dma((chunks,)),
@@ -376,11 +422,17 @@
             collective_id=0, has_side_effects=True, vmem_limit_bytes=60 * 1024 * 1024
         ),
     )(
-        layer_input, output_grad, route_ids, route_probs,
+        layer_input, output_grad, route_ids.T, route_probs.T,
         gate_weight[0], up_weight[0], down_weight[0],
     )
-    xgrad, pgrad, ggrad, ugrad, dgrad = outs
-    return (xgrad, pgrad, ggrad[None], ugrad[None], dgrad[None])
+    xgrad, pgrad, ggrad, ugrad, dgrad = pl.pallas_call(
+        copy_out,
+        out_shape=out_shape,
+        in_specs=[anyw] * 5,
+        out_specs=[anyw] * 5,
+        scratch_shapes=[pltpu.VMEM(o.shape, o.dtype) for o in out_shape] + [dma((5,)), dma((5,))],
+    )(*outs)
+    return (xgrad, pgrad.T, ggrad[None], ugrad[None], dgrad[None])
 
 
 def solution(mesh, sizes=(4, 8, 8)):

time: 91.9 us -> 89.4 us (0.973)
  local copies, waits for them, and re-layouts: 7.96 us -> 0 us
  Pallas kernels: 82.9 us -> 88.6 us
    unnamed x17 -> x0, local copies, waits for them, and re-layouts: 7.96 us -> none
    pallas_call x1 -> x2, Pallas kernels: 82.9 us -> 88.6 us  [the longest x1 86.3 us: on_device(): pl.pallas_call(functools.partial(kernel, nx, ny, nz), out_shape=out_shape...]
where the time goes in v2:
time: 89.4 us; the launch traced here: 89.2 us
  Pallas kernels  88.6 us (99%)
    pallas_call x1, Pallas kernels, on_device(): pl.pallas_call(functools.partial(kernel, nx, ny, nz), out_shape=out_shape...  86.3 us
    pallas_call x1, Pallas kernels, on_device(): pl.pallas_call(copy_out, out_shape=out_shape, in_specs=[anyw] * 5, out_sp...  2.29 us

profile of v2, /device:TPU:1, one launch (start us, length us, event | category | flops | bytes accessed | tf_op | source)
XLA Modules:
  0.0 89.2 jit_solution(7585993229806957969)
XLA Ops:
  0.6 86.3 %shard_map.110 = (bf16[40,256]{1,0:T(8,128)(2,1)}, bf16[8,40]{1,0:T(8,128)(2,1)}, bf16[256,1024]{1,0:T(8,128)(2,1)}, bf16[256,1024]{1,0:T(8,128)(2,1)}, bf16[1024,256]{1,0:T(8,128)(2,1)}) custom-call(bf16[40,256]{1,0:T(8,128)(2,1)} %x_ref.1, bf16[40,256]{1,0:T(8,128)(2,1)} %g_ref.1, s32[8,40]{1,0:T(8,128)} %bitcast.12, bf16[8,40]{1,0:T(8,128)(2,1)} %bitcast.13, ...), custom_call_target="tpu_custom_call" | custom-call | tf_op jit(solution)/shard_map/pallas_call | solution.py:386
  86.9 2.3 %shard_map.111 = (bf16[40,256]{1,0:T(8,128)(2,1)}, bf16[8,40]{1,0:T(8,128)(2,1)}, bf16[256,1024]{1,0:T(8,128)(2,1)}, bf16[256,1024]{1,0:T(8,128)(2,1)}, bf16[1024,256]{1,0:T(8,128)(2,1)}) custom-call(bf16[40,256]{1,0:T(8,128)(2,1)} %get-tuple-element.15.refs_0_, bf16[8,40]{1,0:T(8,128)(2,1)} %get-tuple-element.16.refs_1_, ...), custom_call_target="tpu_custom_call" | custom-call | tf_op jit(solution)/shard_map/pallas_call | solution.py:428

commit v3 on v2

--- a/solution.py
+++ b/solution.py
@@ -12,12 +12,6 @@
 F32 = jnp.float32
 BLK = 16
 LANE = 128
-PLAN = (
-    (0, 0), (1, 0), (0, 1), (2, 0), (1, 1), (3, 0), (0, 2), (4, 0), (2, 1), (1, 2), (5, 0), (3, 1), (2, 2), (0, 3),
-    (6, 0), (1, 3), (4, 1), (3, 2), (2, 3), (7, 0), (5, 1), (4, 2), (3, 3), (8, 0), (6, 1), (5, 2), (4, 3),
-    (9, 0), (7, 1), (6, 2), (5, 3), (8, 1), (7, 2), (6, 3), (10, 0), (9, 1), (8, 2), (7, 3), (10, 1), (9, 2), (8, 3),
-    (10, 2), (9, 3), (10, 3),
-)
 
 
 def log2(n):
@@ -154,7 +148,7 @@
     pl.semaphore_wait(barrier, slots - 1 + 3)
 
     def w_copy(i):
-        src, dst = ((gate_hbm, pgw), (up_hbm, puw), (down_hbm, pdw))[i]
+        src, dst = ((gw_ref, pgw), (uw_ref, puw), (dw_ref, pdw))[i]
         return remote(src, dst, w_s.at[i], w_r.at[i], other)
 
     def block(q):
@@ -167,6 +161,7 @@
         return remote(rgrad.at[block(q)], back.at[block(q)], ret_s.at[q], ret_r.at[q], origin(q))
 
     for i in range(3):
+        load(i).wait()
         w_copy(i).start()
 
     @pl.loop(1, slots)
@@ -220,7 +215,6 @@
         fwd_copy(k).wait_recv()
         if k == 0:
             for i in range(3):
-                load(i).wait()
                 w_copy(i).wait_recv()
         x0, g0, col = split_rows(recv[half_rows(k, core), :], width)
         x1, g1, _ = split_rows(peer[k], width)
@@ -297,8 +291,10 @@
     stages += [swiglu]
     stages += [functools.partial(lambda k, h: ag_hop(k, h), h=h) for h in range(ha)]
     stages += [give_back]
-    for stage, k in PLAN:
-        stages[stage](k)
+    for tick in range(len(stages) + chunks - 1):
+        for k in range(chunks):
+            if 0 <= tick - k < len(stages):
+                stages[tick - k](k)
 
     xs, gs, col = split_rows(recv[...], width)
     scaled = (gs.astype(F32) * col).astype(BF)
@@ -372,7 +368,6 @@
     hops = nz - 1
     assert hidden == nz * LANE
     assert 3 * toks * topk // (2 * slots) < BLK
-    assert (chunks, nz) == (4, 8)
     vmem = pl.BlockSpec(memory_space=pltpu.VMEM)
     anyw = pl.BlockSpec(memory_space=pl.ANY)
     dma = pltpu.SemaphoreType.DMA

time: 89.4 us -> 85.2 us (0.953)
  Pallas kernels: 88.6 us -> 84.3 us
    pallas_call x1, Pallas kernels: 86.3 us -> 82 us  [on_device(): pl.pallas_call(functools.partial(kernel, nx, ny, nz), out_shape=out_shape...]
where the time goes in v3:
time: 85.2 us; the launch traced here: 85 us
  Pallas kernels  84.3 us (99%)
    pallas_call x1, Pallas kernels, on_device(): pl.pallas_call(functools.partial(kernel, nx, ny, nz), out_shape=out_shape...  82 us
    pallas_call x1, Pallas kernels, on_device(): pl.pallas_call(copy_out, out_shape=out_shape, in_specs=[anyw] * 5, out_sp...  2.29 us

profile of v3, /device:TPU:1, one launch (start us, length us, event | category | flops | bytes accessed | tf_op | source)
XLA Modules:
  0.0 85.0 jit_solution(1582674652361702495)
XLA Ops:
  0.6 82.0 %shard_map.110 = (bf16[40,256]{1,0:T(8,128)(2,1)}, bf16[8,40]{1,0:T(8,128)(2,1)}, bf16[256,1024]{1,0:T(8,128)(2,1)}, bf16[256,1024]{1,0:T(8,128)(2,1)}, bf16[1024,256]{1,0:T(8,128)(2,1)}) custom-call(bf16[40,256]{1,0:T(8,128)(2,1)} %x_ref.1, bf16[40,256]{1,0:T(8,128)(2,1)} %g_ref.1, s32[8,40]{1,0:T(8,128)} %bitcast.12, bf16[8,40]{1,0:T(8,128)(2,1)} %bitcast.13, ...), custom_call_target="tpu_custom_call" | custom-call | tf_op jit(solution)/shard_map/pallas_call | solution.py:381
  82.7 2.3 %shard_map.111 = (bf16[40,256]{1,0:T(8,128)(2,1)}, bf16[8,40]{1,0:T(8,128)(2,1)}, bf16[256,1024]{1,0:T(8,128)(2,1)}, bf16[256,1024]{1,0:T(8,128)(2,1)}, bf16[1024,256]{1,0:T(8,128)(2,1)}) custom-call(bf16[40,256]{1,0:T(8,128)(2,1)} %get-tuple-element.15.refs_0_, bf16[8,40]{1,0:T(8,128)(2,1)} %get-tuple-element.16.refs_1_, ...), custom_call_target="tpu_custom_call" | custom-call | tf_op jit(solution)/shard_map/pallas_call | solution.py:423

commit v4 on v3

--- a/solution.py
+++ b/solution.py
@@ -70,9 +70,13 @@
     fore, aft = zdev(1), zdev(-1)
     other = {"dp": z * 2 + 1 - core}
 
+    def reach(c):
+        return jnp.where(c == chunks - 1, 1, jnp.where(c == 0, 0, c + 1))
+
     def offset(q):
         c, b, dx = q // per, (q // nx) % 2, q % nx
-        dy = jnp.where(b == 0, -c, c + 1)
+        far = reach(c)
+        dy = jnp.where(b == 0, -far, far + 1)
         return dx, dy
 
     def target(q):
@@ -111,7 +115,7 @@
 
     q_lane = iota((toks, slots), 1)
     c_l, b_l, dx_l = q_lane >> (lx + 1), (q_lane >> lx) & 1, q_lane & (nx - 1)
-    dy_l = jnp.where(b_l == 0, -c_l, c_l + 1)
+    dy_l = jnp.where(b_l == 0, -reach(c_l), reach(c_l) + 1)
     named = (((mx + dx_l) & (nx - 1)) * ny + ((my + dy_l) & (ny - 1))).astype(F32)
     eye = jnp.where(iota((toks, toks), 0) == iota((toks, toks), 1), 1.0, 0.0).astype(BF)
     ids = dot(eye, ids_ref[...].astype(F32).astype(BF), 1, 1)

time: 85.2 us -> 83.1 us (0.975)
  Pallas kernels: 84.3 us -> 82.2 us
    pallas_call x1, Pallas kernels: 82 us -> 79.9 us  [on_device(): pl.pallas_call(functools.partial(kernel, nx, ny, nz), out_shape=out_shape...]
where the time goes in v4:
time: 83.1 us; the launch traced here: 82.9 us
  Pallas kernels  82.2 us (99%)
    pallas_call x1, Pallas kernels, on_device(): pl.pallas_call(functools.partial(kernel, nx, ny, nz), out_shape=out_shape...  79.9 us
    pallas_call x1, Pallas kernels, on_device(): pl.pallas_call(copy_out, out_shape=out_shape, in_specs=[anyw] * 5, out_sp...  2.29 us

profile of v4, /device:TPU:1, one launch (start us, length us, event | category | flops | bytes accessed | tf_op | source)
XLA Modules:
  0.0 82.9 jit_solution(6208925564725781012)
XLA Ops:
  0.6 79.9 %shard_map.110 = (bf16[40,256]{1,0:T(8,128)(2,1)}, bf16[8,40]{1,0:T(8,128)(2,1)}, bf16[256,1024]{1,0:T(8,128)(2,1)}, bf16[256,1024]{1,0:T(8,128)(2,1)}, bf16[1024,256]{1,0:T(8,128)(2,1)}) custom-call(bf16[40,256]{1,0:T(8,128)(2,1)} %x_ref.1, bf16[40,256]{1,0:T(8,128)(2,1)} %g_ref.1, s32[8,40]{1,0:T(8,128)} %bitcast.12, bf16[8,40]{1,0:T(8,128)(2,1)} %bitcast.13, ...), custom_call_target="tpu_custom_call" | custom-call | tf_op jit(solution)/shard_map/pallas_call | solution.py:385
  80.6 2.3 %shard_map.111 = (bf16[40,256]{1,0:T(8,128)(2,1)}, bf16[8,40]{1,0:T(8,128)(2,1)}, bf16[256,1024]{1,0:T(8,128)(2,1)}, bf16[256,1024]{1,0:T(8,128)(2,1)}, bf16[1024,256]{1,0:T(8,128)(2,1)}) custom-call(bf16[40,256]{1,0:T(8,128)(2,1)} %get-tuple-element.15.refs_0_, bf16[8,40]{1,0:T(8,128)(2,1)} %get-tuple-element.16.refs_1_, ...), custom_call_target="tpu_custom_call" | custom-call | tf_op jit(solution)/shard_map/pallas_call | solution.py:427
